TPU v7x, 512 devices: a whole 4x4x16 slice. The times are simulated.
512 devices in a mesh: dp: 32 (over y, x, core), mp: 16 (over z).
Axes of the slice: x: 4, y: 4, z: 16, core: 2. Of those that a mesh axis runs over, the one named last changes fastest.
Arguments:
- tokens: bfloat16 [32768, 8192], P('dp', 'mp'), may hold values from -6 to 6
- value_weight: bfloat16 [8192, 1024], P('mp'), may hold values from -0.0625 to 0.0625
- down_panels: bfloat16 [256, 8192, 64], P('dp', 'mp'), may hold values from -0.0625 to 0.0625
- up_panels: bfloat16 [256, 64, 1024], P('dp'), may hold values from -0.75 to 0.75
- cotangent: bfloat16 [32768, 1024], P(('dp', 'mp')), may hold values from -6 to 6
- block_adapter: int32 [256], replicated, may hold values from 0 to 255, as said below
- adapter_slot: int32 [256], replicated, may hold values from 0 to 255, as said below
Outputs:
- projected: bfloat16 [32768, 1024], P(('dp', 'mp'))
- grad_tokens: bfloat16 [32768, 8192], P('dp', 'mp')
- grad_down: bfloat16 [256, 8192, 64], P('dp', 'mp')
- grad_up: bfloat16 [256, 64, 1024], P('dp')
Inputs may be any that keep to these rules, and one draw needn't show every extreme that they name: `block_adapter`: the 8 blocks of one index of dp name adapters stored on 8 different owners, the owner of slot s being s // 8. `adapter_slot`: A permutation of the adapters.
All inputs are finite; a program needn't handle non-finite values.
Results may differ from a plain program's by a relative error of at most 0.005.
Values may be sent and summed in bfloat16 or wider, within the bound.
A program may use at most 128 MiB of HBM per device.

v0:
```python
import jax
import jax.numpy as jnp
from jax import lax
from jax.sharding import PartitionSpec as P

RANK = 64
BLOCK_ROWS = 128


def per_device(
    tokens, value_weight, down_panels, up_panels, cotangent, block_adapter, adapter_slot
):
    n_owners = lax.axis_size("dp")
    myself = lax.axis_index("dp")
    n_split = lax.axis_size("mp")
    my_part = lax.axis_index("mp")
    rows, width_dev = tokens.shape
    own_rows, kv_full = cotangent.shape
    kv_part = kv_full // n_split
    stored = down_panels.shape[0]
    blocks = rows // BLOCK_ROWS
    hits = block_adapter[:, None] == jnp.arange(adapter_slot.shape[0], dtype=jnp.int32)[None, :]
    slots_all = jnp.sum(jnp.where(hits, adapter_slot[None, :], 0), axis=1)
    owner_all = (slots_all // stored).reshape(n_owners, blocks)
    local_all = (slots_all % stored).reshape(n_owners, blocks)
    mine = owner_all == myself
    wanted = jnp.sum(jnp.where(mine, local_all, 0), axis=1)
    served = jnp.any(mine, axis=1)
    pick_mask = (wanted[:, None] == jnp.arange(stored, dtype=jnp.int32)[None, :]) & served[:, None]
    my_owner = lax.dynamic_index_in_dim(owner_all, myself, 0, keepdims=False)
    select_mask = my_owner[:, None] == jnp.arange(n_owners, dtype=jnp.int32)[None, :]
    up_cols = lax.dynamic_slice_in_dim(up_panels, my_part * kv_part, kv_part, 2)
    both = jnp.concatenate([down_panels, up_cols], axis=1)
    got = lax.all_to_all(
        jnp.take(both, wanted, axis=0), "dp", split_axis=0, concat_axis=0, tiled=True
    )
    mine_got = jnp.take(got, my_owner, axis=0)
    panel_a = mine_got[:, :width_dev]
    panel_b_cols = mine_got[:, width_dev:]
    cot_all = lax.all_gather(cotangent, "mp", axis=0, tiled=True)
    panel_b = lax.all_gather(panel_b_cols, "mp", axis=2, tiled=True)
    token_blocks = tokens.reshape(blocks, BLOCK_ROWS, width_dev)
    partial_value = jnp.dot(tokens, value_weight, preferred_element_type=jnp.float32)
    base = lax.psum_scatter(partial_value, "mp", scatter_dimension=0, tiled=True)
    down_part = jnp.einsum(
        "bnd,bdk->bnk", token_blocks, panel_a, preferred_element_type=jnp.float32
    )
    first_row = my_part * own_rows
    my_down = lax.psum_scatter(
        down_part.reshape(rows, RANK), "mp", scatter_dimension=0, tiled=True
    ).astype(jnp.bfloat16)
    down = lax.all_gather(my_down, "mp", axis=0, tiled=True)
    cot_blocks = cot_all.reshape(blocks, BLOCK_ROWS, kv_full)
    back = jnp.einsum(
        "bnc,bkc->bnk", cot_blocks, panel_b, preferred_element_type=jnp.float32
    ).astype(jnp.bfloat16)
    block_grad_a = jnp.einsum(
        "bnd,bnk->bdk", token_blocks, back, preferred_element_type=jnp.float32
    ).astype(jnp.bfloat16)
    cot_share = lax.dynamic_slice_in_dim(cot_blocks, my_part * kv_part, kv_part, 2)
    block_grad_b = jnp.einsum(
        "bnk,bnc->bkc",
        down.reshape(blocks, BLOCK_ROWS, RANK),
        cot_share,
        preferred_element_type=jnp.float32,
    ).astype(jnp.bfloat16)
    grads = jnp.concatenate([block_grad_a, block_grad_b], axis=1)
    send_g = jnp.einsum(
        "bo,bdk->odk", select_mask.astype(jnp.bfloat16), grads, preferred_element_type=jnp.float32
    ).astype(jnp.bfloat16)
    recv_g = lax.all_to_all(send_g, "dp", split_axis=0, concat_axis=0, tiled=True)
    grad_both = jnp.einsum(
        "ra,rdk->adk", pick_mask.astype(jnp.bfloat16), recv_g, preferred_element_type=jnp.float32
    ).astype(jnp.bfloat16)
    grad_down = grad_both[:, :width_dev]
    grad_up = lax.all_gather(grad_both[:, width_dev:], "mp", axis=2, tiled=True)
    my_up = lax.dynamic_index_in_dim(panel_b, first_row // BLOCK_ROWS, 0, keepdims=False)
    lifted = jnp.dot(my_down, my_up, preferred_element_type=jnp.float32)
    projected = (base + lifted).astype(jnp.bfloat16)
    grad_base = jnp.einsum("nc,dc->nd", cot_all, value_weight, preferred_element_type=jnp.float32)
    through = jnp.einsum("bnk,bdk->bnd", back, panel_a, preferred_element_type=jnp.float32)
    grad_tokens = (grad_base + through.reshape(rows, width_dev)).astype(jnp.bfloat16)
    return (projected, grad_tokens, grad_down, grad_up)


def solution(mesh):
    placed = (
        P("dp", "mp"),
        P("mp", None),
        P("dp", "mp", None),
        P("dp", None, None),
        P(("dp", "mp"), None),
        P(),
        P(),
    )
    return jax.shard_map(
        per_device,
        mesh=mesh,
        in_specs=placed,
        out_specs=(P(("dp", "mp"), None), P("dp", "mp"), P("dp", "mp", None), P("dp", None, None)),
        check_vma=False,
    )
```

profile of v0, /device:TPU:2, one launch (start us, length us, event | category | flops | bytes accessed | tf_op | source)
XLA Modules:
  0.0 442.6 jit_solution(5169202900593899612)
XLA Ops:
  7.2 1.0 select_reduce_fusion
  8.5 1.0 constant_dynamic-slice_fusion
  9.7 1.1 pad_maximum_fusion
  10.8 2.4 gather_fusion
  13.2 3.6 broadcast_select_fusion
  16.8 10.3 %all-to-all-start = ((bf16[32,576,64]{1,2,0:T(8,128)(2,1)}), bf16[32,576,64]{1,2,0:T(8,128)(2,1)}, u32[]{:S(2)}, u32[]{:S(2)}) async-start(bf16[32,576,64]{1,2,0:T(8,128)(2,1)} %broadcast_select_fusion), calls=%async_computation.1 | async-start | bytes 5242880 | tf_op jit(solution)/shard_map/all_to_all | solution.py:34
  27.2 33.9 %all-to-all-done = bf16[32,576,64]{1,2,0:T(8,128)(2,1)} async-done(((bf16[32,576,64]{1,2,0:T(8,128)(2,1)}), bf16[32,576,64]{1,2,0:T(8,128)(2,1)}, u32[]{:S(2)}, u32[]{:S(2)}) %all-to-all-start) | async-done | bytes 2359328 | tf_op jit(solution)/shard_map/all_to_all | solution.py:34
  61.1 2.4 gather_fusion.1
  64.1 1.0 copy.60
  66.7 4.4 fusion.34
  71.2 62.2 %reduce-scatter.7.cloned.1.call-done = f32[64,64]{1,0:T(8,128)} async-done(((f32[1024,64]{1,0:T(8,128)}), f32[64,64]{1,0:T(8,128)}) %reduce-scatter.7.cloned.1.call-update) | async-done | bytes 16400
  134.3 29.0 %all_gather.14 = bf16[1024,64]{1,0:T(8,128)(2,1)S(1)} all-gather(bf16[64,64]{1,0:T(8,128)(2,1)S(1)} %copy.45), channel_id=1, replica_groups=mesh['dp'=32,'mp'=16] {'mp'}, dimensions={0}, use_global_device_ids=true | all-gather | bytes 139264 | tf_op jit(solution)/shard_map/all_gather | solution.py:52
  163.3 43.5 %all-gather.6.cloned.1.call-done = bf16[1024,1024]{1,0:T(8,128)(2,1)} async-done(((bf16[64,1024]{1,0:T(8,128)(2,1)}), bf16[1024,1024]{1,0:T(8,128)(2,1)}) %all-gather.6.cloned.1.call-update) | async-done | bytes 2097168 | tf_op jit(solution)/shard_map/all_gather | solution.py:40
  206.8 1.3 convolution_convert_fusion.2
  208.1 71.3 %all-gather.4.cloned.1.call-done = bf16[8,64,1024]{1,2,0:T(8,128)(2,1)} async-done(((bf16[8,64,64]{1,2,0:T(8,128)(2,1)}), bf16[8,64,1024]{1,2,0:T(8,128)(2,1)}) %all-gather.4.cloned.1.call-update) | async-done | bytes 1048592 | tf_op jit(solution)/shard_map/all_gather | solution.py:41
  279.4 3.1 convolution_convert_fusion.3
  284.8 40.2 %all_to_all.10 = bf16[32,576,64]{1,2,0:T(8,128)(2,1)S(1)} all-to-all(bf16[32,576,64]{1,2,0:T(8,128)(2,1)S(1)} %copy.50), channel_id=1, replica_groups=mesh['dp'=32,'mp'=16] {'dp'}, dimensions={0} | all-to-all | bytes 4718592 | tf_op jit(solution)/shard_map/all_to_all | solution.py:71
  325.0 1.8 fusion.3
  328.1 1.1 copy-done.1
  329.2 2.3 fusion.2
  332.5 26.8 %reduce-scatter.5.cloned.1.call-done = f32[64,1024]{1,0:T(8,128)} async-done(((f32[1024,1024]{1,0:T(8,128)}), f32[64,1024]{1,0:T(8,128)}) %reduce-scatter.5.cloned.1.call-update) | async-done | bytes 262160 | tf_op jit(solution)/shard_map/reduce_scatter | solution.py:44
  359.2 1.9 fusion.7
  361.2 71.6 %all-gather.8.cloned.1.call-done = bf16[8,64,1024]{1,0,2:T(8,128)(2,1)} async-done(((bf16[8,64,64]{1,0,2:T(8,128)(2,1)}), bf16[8,64,1024]{1,0,2:T(8,128)(2,1)}) %all-gather.8.cloned.1.call-update) | async-done | bytes 1048592 | tf_op jit(solution)/shard_map/all_gather | solution.py:76
  432.8 3.3 copy.53
  (38 shorter events, 8.2 us)
Async XLA Ops:
  7.2 56.5 %copy-start = (bf16[1024,512]{1,0:T(8,128)(2,1)S(1)}, bf16[1024,512]{1,0:T(8,128)(2,1)}, u32[]{:S(2)}) copy-start(bf16[1024,512]{1,0:T(8,128)(2,1)} %param.7) | copy-start | bytes 3145732
  16.8 44.3 %all-to-all-start = ((bf16[32,576,64]{1,2,0:T(8,128)(2,1)}), bf16[32,576,64]{1,2,0:T(8,128)(2,1)}, u32[]{:S(2)}, u32[]{:S(2)}) async-start(bf16[32,576,64]{1,2,0:T(8,128)(2,1)} %broadcast_select_fusion), calls=%async_computation.1 | async-start | bytes 5242880 | tf_op jit(solution)/shard_map/all_to_all | solution.py:34
  27.1 106.3 %reduce-scatter.7.cloned.1.call-start = ((), (), s32[]{:S(2)}) async-start(), calls=%async_computation.8 | async-start | bytes 557056
  65.1 141.6 %all-gather.6.cloned.1.call-start = ((), (), s32[]{:S(2)}) async-start(), calls=%async_computation.6 | async-start | bytes 2228224 | tf_op jit(solution)/shard_map/all_gather | solution.py:40
  65.9 213.5 %all-gather.4.cloned.1.call-start = ((), (), s32[]{:S(2)}) async-start(), calls=%async_computation.5 | async-start | bytes 2228224 | tf_op jit(solution)/shard_map/all_gather | solution.py:41
  66.6 292.6 %reduce-scatter.5.cloned.1.call-start = ((), (), s32[]{:S(2)}) async-start(), calls=%async_computation.4 | async-start | bytes 4456448 | tf_op jit(solution)/shard_map/reduce_scatter | solution.py:44
  71.1 361.6 %all-gather.8.cloned.1.call-start = ((), (), s32[]{:S(2)}) async-start(), calls=%async_computation.7 | async-start | bytes 2228224 | tf_op jit(solution)/shard_map/all_gather | solution.py:76
  326.8 1.3 copy-start.2
  327.5 1.7 copy-start.1
Sparse Core Ops, SparseCore 0:
  65.3 68.0 reduce-scatter.6
  135.7 71.0 all-gather.5
  209.7 69.7 all-gather.3
  282.4 76.8 reduce-scatter.4
  362.0 70.7 all-gather.7
where the time goes:
time: 443 us
  waiting for transfers between devices  310 us (70%)
  blocking collectives  69.2 us (16%)
  matrix products  17 us (4%)
  local copies, waits for them, and re-layouts  15.7 us (4%)
  between operations  14 us (3%)
  starting transfers between devices  10.5 us (2%)
  other arithmetic  6.2 us (1%)
    all_gather x1, waiting for transfers between devices, per_device(): grad_up = lax.all_gather(grad_both[:, width_dev:], 'mp', axis=2, tiled=True)  71.6 us
    all_gather x1, waiting for transfers between devices, per_device(): panel_b = lax.all_gather(panel_b_cols, 'mp', axis=2, tiled=True)  71.3 us
    unnamed x6, waiting for transfers between devices  62.9 us
    all_gather x1, waiting for transfers between devices, per_device(): cot_all = lax.all_gather(cotangent, 'mp', axis=0, tiled=True)  43.5 us
    all_to_all x1, blocking collectives, per_device(): lax.all_to_all(send_g, 'dp', split_axis=0, concat_axis=0, tiled=True)  40.2 us
    all_to_all x1, waiting for transfers between devices, per_device(): lax.all_to_all(jnp.take(both, wanted, axis=0), 'dp', split_axis=0, concat...  33.9 us
    all_gather x1, blocking collectives, per_device(): down = lax.all_gather(my_down, 'mp', axis=0, tiled=True)  29 us
    reduce_scatter x1, waiting for transfers between devices, per_device(): lax.psum_scatter(partial_value, 'mp', scatter_dimension=0, tiled=True)  26.8 us
  transfers between devices with their start and end apart: 6, of which 6 were waited for; matrix products, arithmetic and copies ran while one was open for 5% of the time, Pallas kernels for 0%

commit v1 on v0

--- a/solution.py
+++ b/solution.py
@@ -37,7 +37,12 @@
     mine_got = jnp.take(got, my_owner, axis=0)
     panel_a = mine_got[:, :width_dev]
     panel_b_cols = mine_got[:, width_dev:]
-    cot_all = lax.all_gather(cotangent, "mp", axis=0, tiled=True)
+    ring = [cotangent]
+    for hop in range(15):
+        ring.append(lax.ppermute(ring[-1], "mp", [(dev, (dev + 1) % 16) for dev in range(16)]))
+    cot_all = jnp.roll(
+        jnp.concatenate(ring[::-1], axis=0), (lax.axis_index("mp") + 1) * ring[0].shape[0], axis=0
+    )
     panel_b = lax.all_gather(panel_b_cols, "mp", axis=2, tiled=True)
     token_blocks = tokens.reshape(blocks, BLOCK_ROWS, width_dev)
     partial_value = jnp.dot(tokens, value_weight, preferred_element_type=jnp.float32)

time: 443 us -> 373 us (0.84)
  waiting for transfers between devices: 310 us -> 210 us
  starting transfers between devices: 10.5 us -> 39.1 us
    ppermute x0 -> x15, waiting for transfers between devices: none -> 104 us  [per_device(): lax.ppermute(ring[-1], 'mp', [(dev, (dev + 1) % 16) for dev in range(16)])]
    all_gather x1, waiting for transfers between devices: 71.3 us -> 0.02 us  [per_device(): panel_b = lax.all_gather(panel_b_cols, 'mp', axis=2, tiled=True)]
    unnamed x6 -> x5, waiting for transfers between devices: 62.9 us -> 0.09 us
    all_gather x1 -> x0, waiting for transfers between devices: 43.5 us -> none  [per_device(): cot_all = lax.all_gather(cotangent, 'mp', axis=0, tiled=True)]
    ppermute x0 -> x15, starting transfers between devices: none -> 28.6 us  [per_device(): lax.ppermute(ring[-1], 'mp', [(dev, (dev + 1) % 16) for dev in range(16)])]
    reduce_scatter x1, waiting for transfers between devices: 26.8 us -> 0.95 us  [per_device(): lax.psum_scatter(partial_value, 'mp', scatter_dimension=0, tiled=True)]
  transfers between devices with their start and end apart: 6 -> 20, of which waited for: 6 -> 18; matrix products, arithmetic and copies ran while one was open for 5% -> 6% of each run, Pallas kernels for 0% -> 0%
where the time goes in v1:
time: 373 us; the launch traced here: 372 us
  waiting for transfers between devices  210 us (56%)
  blocking collectives  68 us (18%)
  starting transfers between devices  39.1 us (10%)
  matrix products  17.8 us (5%)
  local copies, waits for them, and re-layouts  16 us (4%)
  between operations  14.4 us (4%)
  other arithmetic  6.23 us (2%)
    ppermute x15, waiting for transfers between devices, per_device(): lax.ppermute(ring[-1], 'mp', [(dev, (dev + 1) % 16) for dev in range(16)])  104 us
    all_gather x1, waiting for transfers between devices, per_device(): grad_up = lax.all_gather(grad_both[:, width_dev:], 'mp', axis=2, tiled=True)  71.5 us
    all_to_all x1, blocking collectives, per_device(): lax.all_to_all(send_g, 'dp', split_axis=0, concat_axis=0, tiled=True)  40.1 us
    all_to_all x1, waiting for transfers between devices, per_device(): lax.all_to_all(jnp.take(both, wanted, axis=0), 'dp', split_axis=0, concat...  33.9 us
    ppermute x15, starting transfers between devices, per_device(): lax.ppermute(ring[-1], 'mp', [(dev, (dev + 1) % 16) for dev in range(16)])  28.6 us
    all_gather x1, blocking collectives, per_device(): down = lax.all_gather(my_down, 'mp', axis=0, tiled=True)  27.8 us
    all_to_all x1, starting transfers between devices, per_device(): lax.all_to_all(jnp.take(both, wanted, axis=0), 'dp', split_axis=0, concat...  10.3 us
  transfers between devices with their start and end apart: 20, of which 18 were waited for; matrix products, arithmetic and copies ran while one was open for 6% of the time, Pallas kernels for 0%

profile of v1, /device:TPU:2, one launch (start us, length us, event | category | flops | bytes accessed | tf_op | source)
XLA Modules:
  0.0 371.5 jit_solution(7375124786495941900)
XLA Ops:
  13.2 3.6 broadcast_select_fusion
  16.8 10.3 %all-to-all-start = ((bf16[32,576,64]{1,2,0:T(8,128)(2,1)}), bf16[32,576,64]{1,2,0:T(8,128)(2,1)}, u32[]{:S(2)}, u32[]{:S(2)}) async-start(bf16[32,576,64]{1,2,0:T(8,128)(2,1)} %broadcast_select_fusion), calls=%async_computation.1 | async-start | bytes 5242880 | tf_op jit(solution)/shard_map/all_to_all | solution.py:34
  27.3 33.9 %all-to-all-done = bf16[32,576,64]{1,2,0:T(8,128)(2,1)} async-done(((bf16[32,576,64]{1,2,0:T(8,128)(2,1)}), bf16[32,576,64]{1,2,0:T(8,128)(2,1)}, u32[]{:S(2)}, u32[]{:S(2)}) %all-to-all-start) | async-done | bytes 2359328 | tf_op jit(solution)/shard_map/all_to_all | solution.py:34
  67.9 9.7 %collective-permute-done = bf16[64,1024]{1,0:T(8,128)(2,1)S(1)} collective-permute-done((bf16[64,1024]{1,0:T(8,128)(2,1)S(1)}, bf16[64,1024]{1,0:T(8,128)(2,1)S(1)}, u32[]{:S(2)}, u32[]{:S(2)}) %collective-permute-start) | collective-permute-done | bytes 131104 | tf_op jit(solution)/shard_map/ppermute | solution.py:42
  79.6 6.5 %collective-permute-done.1 = bf16[64,1024]{1,0:T(8,128)(2,1)S(1)} collective-permute-done((bf16[64,1024]{1,0:T(8,128)(2,1)S(1)}, bf16[64,1024]{1,0:T(8,128)(2,1)S(1)}, u32[]{:S(2)}, u32[]{:S(2)}) %collective-permute-start.1) | collective-permute-done | bytes 131104 | tf_op jit(solution)/shard_map/ppermute | solution.py:42
  88.0 6.3 %collective-permute-done.2 = bf16[64,1024]{1,0:T(8,128)(2,1)S(1)} collective-permute-done((bf16[64,1024]{1,0:T(8,128)(2,1)S(1)}, bf16[64,1024]{1,0:T(8,128)(2,1)S(1)}, u32[]{:S(2)}, u32[]{:S(2)}) %collective-permute-start.2) | collective-permute-done | bytes 131104 | tf_op jit(solution)/shard_map/ppermute | solution.py:42
  96.2 6.4 %collective-permute-done.3 = bf16[64,1024]{1,0:T(8,128)(2,1)S(1)} collective-permute-done((bf16[64,1024]{1,0:T(8,128)(2,1)S(1)}, bf16[64,1024]{1,0:T(8,128)(2,1)S(1)}, u32[]{:S(2)}, u32[]{:S(2)}) %collective-permute-start.3) | collective-permute-done | bytes 131104 | tf_op jit(solution)/shard_map/ppermute | solution.py:42
  104.5 7.3 %collective-permute-done.4 = bf16[64,1024]{1,0:T(8,128)(2,1)S(1)} collective-permute-done((bf16[64,1024]{1,0:T(8,128)(2,1)S(1)}, bf16[64,1024]{1,0:T(8,128)(2,1)S(1)}, u32[]{:S(2)}, u32[]{:S(2)}) %collective-permute-start.4) | collective-permute-done | bytes 131104 | tf_op jit(solution)/shard_map/ppermute | solution.py:42
  113.7 7.6 %collective-permute-done.5 = bf16[64,1024]{1,0:T(8,128)(2,1)S(1)} collective-permute-done((bf16[64,1024]{1,0:T(8,128)(2,1)S(1)}, bf16[64,1024]{1,0:T(8,128)(2,1)S(1)}, u32[]{:S(2)}, u32[]{:S(2)}) %collective-permute-start.5) | collective-permute-done | bytes 131104 | tf_op jit(solution)/shard_map/ppermute | solution.py:42
  123.3 6.6 %collective-permute-done.6 = bf16[64,1024]{1,0:T(8,128)(2,1)S(1)} collective-permute-done((bf16[64,1024]{1,0:T(8,128)(2,1)S(1)}, bf16[64,1024]{1,0:T(8,128)(2,1)S(1)}, u32[]{:S(2)}, u32[]{:S(2)}) %collective-permute-start.6) | collective-permute-done | bytes 131104 | tf_op jit(solution)/shard_map/ppermute | solution.py:42
  131.8 6.1 %collective-permute-done.7 = bf16[64,1024]{1,0:T(8,128)(2,1)S(1)} collective-permute-done((bf16[64,1024]{1,0:T(8,128)(2,1)S(1)}, bf16[64,1024]{1,0:T(8,128)(2,1)S(1)}, u32[]{:S(2)}, u32[]{:S(2)}) %collective-permute-start.7) | collective-permute-done | bytes 131104 | tf_op jit(solution)/shard_map/ppermute | solution.py:42
  139.9 6.1 %collective-permute-done.8 = bf16[64,1024]{1,0:T(8,128)(2,1)S(1)} collective-permute-done((bf16[64,1024]{1,0:T(8,128)(2,1)S(1)}, bf16[64,1024]{1,0:T(8,128)(2,1)S(1)}, u32[]{:S(2)}, u32[]{:S(2)}) %collective-permute-start.8) | collective-permute-done | bytes 131104 | tf_op jit(solution)/shard_map/ppermute | solution.py:42
  147.9 6.1 %collective-permute-done.9 = bf16[64,1024]{1,0:T(8,128)(2,1)S(1)} collective-permute-done((bf16[64,1024]{1,0:T(8,128)(2,1)S(1)}, bf16[64,1024]{1,0:T(8,128)(2,1)S(1)}, u32[]{:S(2)}, u32[]{:S(2)}) %collective-permute-start.9) | collective-permute-done | bytes 131104 | tf_op jit(solution)/shard_map/ppermute | solution.py:42
  156.0 4.4 %fusion.34 = f32[1024,1024]{1,0:T(8,128)} fusion(bf16[1024,512]{1,0:T(8,128)(2,1)S(1)} %copy-done, bf16[512,1024]{1,0:T(8,128)(2,1)} %param.8), kind=kOutput, calls=%fused_computation.96 | convolution fusion | flops 1073741824 | bytes 6291456 | tf_op jit(solution)/shard_map/dot_general | solution.py:48
  160.5 2.6 collective-permute-done.10
  165.0 8.4 %collective-permute-done.11 = bf16[64,1024]{1,0:T(8,128)(2,1)S(1)} collective-permute-done((bf16[64,1024]{1,0:T(8,128)(2,1)S(1)}, bf16[64,1024]{1,0:T(8,128)(2,1)S(1)}, u32[]{:S(2)}, u32[]{:S(2)}) %collective-permute-start.11) | collective-permute-done | bytes 131104 | tf_op jit(solution)/shard_map/ppermute | solution.py:42
  175.3 9.2 %collective-permute-done.12 = bf16[64,1024]{1,0:T(8,128)(2,1)S(1)} collective-permute-done((bf16[64,1024]{1,0:T(8,128)(2,1)S(1)}, bf16[64,1024]{1,0:T(8,128)(2,1)S(1)}, u32[]{:S(2)}, u32[]{:S(2)}) %collective-permute-start.12) | collective-permute-done | bytes 131104 | tf_op jit(solution)/shard_map/ppermute | solution.py:42
  186.4 7.8 %collective-permute-done.13 = bf16[64,1024]{1,0:T(8,128)(2,1)S(1)} collective-permute-done((bf16[64,1024]{1,0:T(8,128)(2,1)S(1)}, bf16[64,1024]{1,0:T(8,128)(2,1)S(1)}, u32[]{:S(2)}, u32[]{:S(2)}) %collective-permute-start.13) | collective-permute-done | bytes 131104 | tf_op jit(solution)/shard_map/ppermute | solution.py:42
  196.2 6.8 %collective-permute-done.14 = bf16[64,1024]{1,0:T(8,128)(2,1)S(1)} collective-permute-done((bf16[64,1024]{1,0:T(8,128)(2,1)S(1)}, bf16[64,1024]{1,0:T(8,128)(2,1)S(1)}, u32[]{:S(2)}, u32[]{:S(2)}) %collective-permute-start.14) | collective-permute-done | bytes 131104 | tf_op jit(solution)/shard_map/ppermute | solution.py:42
  204.8 27.8 %all_gather.10 = bf16[1024,64]{1,0:T(8,128)(2,1)S(1)} all-gather(bf16[64,64]{1,0:T(8,128)(2,1)S(1)} %copy.45), channel_id=1, replica_groups=mesh['dp'=32,'mp'=16] {'mp'}, dimensions={0}, use_global_device_ids=true | all-gather | bytes 139264 | tf_op jit(solution)/shard_map/all_gather | solution.py:57
  237.7 40.1 %all_to_all.10 = bf16[32,576,64]{1,2,0:T(8,128)(2,1)S(1)} all-to-all(bf16[32,576,64]{1,2,0:T(8,128)(2,1)S(1)} %copy.50), channel_id=1, replica_groups=mesh['dp'=32,'mp'=16] {'dp'}, dimensions={0} | all-to-all | bytes 4718592 | tf_op jit(solution)/shard_map/all_to_all | solution.py:76
  282.8 3.5 fusion.2
  290.2 71.5 %all-gather.5.cloned.1.call-done = bf16[8,64,1024]{1,0,2:T(8,128)(2,1)} async-done(((bf16[8,64,64]{1,0,2:T(8,128)(2,1)}), bf16[8,64,1024]{1,0,2:T(8,128)(2,1)}) %all-gather.5.cloned.1.call-update) | async-done | bytes 1048592 | tf_op jit(solution)/shard_map/all_gather | solution.py:81
  361.7 3.3 copy.53
  (101 shorter events, 54.9 us)
Async XLA Ops:
  7.2 56.5 %copy-start = (bf16[1024,512]{1,0:T(8,128)(2,1)S(1)}, bf16[1024,512]{1,0:T(8,128)(2,1)}, u32[]{:S(2)}) copy-start(bf16[1024,512]{1,0:T(8,128)(2,1)} %param.7) | copy-start | bytes 3145732
  16.8 44.3 %all-to-all-start = ((bf16[32,576,64]{1,2,0:T(8,128)(2,1)}), bf16[32,576,64]{1,2,0:T(8,128)(2,1)}, u32[]{:S(2)}, u32[]{:S(2)}) async-start(bf16[32,576,64]{1,2,0:T(8,128)(2,1)} %broadcast_select_fusion), calls=%async_computation.1 | async-start | bytes 5242880 | tf_op jit(solution)/shard_map/all_to_all | solution.py:34
  27.1 38.9 %copy-start.3 = (bf16[64,1024]{1,0:T(8,128)(2,1)S(1)}, bf16[64,1024]{1,0:T(8,128)(2,1)}, u32[]{:S(2)}) copy-start(bf16[64,1024]{1,0:T(8,128)(2,1)} %param.11) | copy-start | bytes 393220
  27.2 176.6 %reduce-scatter.7.cloned.1.call-start = ((), (), s32[]{:S(2)}) async-start(), calls=%async_computation.7 | async-start | bytes 557056
  63.7 96.7 %copy-start.1 = (bf16[8,576,64]{1,2,0:T(8,128)(2,1)}, bf16[8,576,64]{1,2,0:T(8,128)(2,1)S(1)}, u32[]{:S(2)}) copy-start(bf16[8,576,64]{1,2,0:T(8,128)(2,1)S(1)} %broadcast_select_fusion.1) | copy-start | bytes 1769476
  65.2 167.8 %all-gather.3.cloned.1.call-start = ((), (), s32[]{:S(2)}) async-start(), calls=%async_computation.5 | async-start | bytes 2228224 | tf_op jit(solution)/shard_map/all_gather | solution.py:46
  66.0 222.3 %reduce-scatter.5.cloned.1.call-start = ((), (), s32[]{:S(2)}) async-start(), calls=%async_computation.4 | async-start | bytes 4456448 | tf_op jit(solution)/shard_map/reduce_scatter | solution.py:49
  66.0 11.6 %collective-permute-start = (bf16[64,1024]{1,0:T(8,128)(2,1)S(1)}, bf16[64,1024]{1,0:T(8,128)(2,1)S(1)}, u32[]{:S(2)}, u32[]{:S(2)}) collective-permute-start(bf16[64,1024]{1,0:T(8,128)(2,1)S(1)} %copy-done.3), channel_id=1, source_target_pairs={{0,1},{1,2},{2,3},{3,4},{4,5},{5,6},{6,7},{7,8},{8,9},{9,10},{10,1... | collective-permute-start | bytes 393224 | tf_op jit(solution)/shard_map/ppermute | solution.py:42
  77.6 8.4 %collective-permute-start.1 = (bf16[64,1024]{1,0:T(8,128)(2,1)S(1)}, bf16[64,1024]{1,0:T(8,128)(2,1)S(1)}, u32[]{:S(2)}, u32[]{:S(2)}) collective-permute-start(bf16[64,1024]{1,0:T(8,128)(2,1)S(1)} %collective-permute-done), channel_id=1, source_target_pairs={{0,1},{1,2},{2,3},{3,4},{4,5},{5,6},{6,7},{7,8},{8,9},{9,10},{10,1... | collective-permute-start | bytes 393224 | tf_op jit(solution)/shard_map/ppermute | solution.py:42
  86.0 8.2 %collective-permute-start.2 = (bf16[64,1024]{1,0:T(8,128)(2,1)S(1)}, bf16[64,1024]{1,0:T(8,128)(2,1)S(1)}, u32[]{:S(2)}, u32[]{:S(2)}) collective-permute-start(bf16[64,1024]{1,0:T(8,128)(2,1)S(1)} %collective-permute-done.1), channel_id=1, source_target_pairs={{0,1},{1,2},{2,3},{3,4},{4,5},{5,6},{6,7},{7,8},{8,9},{9,10},{10,1... | collective-permute-start | bytes 393224 | tf_op jit(solution)/shard_map/ppermute | solution.py:42
  94.2 8.3 %collective-permute-start.3 = (bf16[64,1024]{1,0:T(8,128)(2,1)S(1)}, bf16[64,1024]{1,0:T(8,128)(2,1)S(1)}, u32[]{:S(2)}, u32[]{:S(2)}) collective-permute-start(bf16[64,1024]{1,0:T(8,128)(2,1)S(1)} %collective-permute-done.2), channel_id=1, source_target_pairs={{0,1},{1,2},{2,3},{3,4},{4,5},{5,6},{6,7},{7,8},{8,9},{9,10},{10,1... | collective-permute-start | bytes 393224 | tf_op jit(solution)/shard_map/ppermute | solution.py:42
  102.6 9.3 %collective-permute-start.4 = (bf16[64,1024]{1,0:T(8,128)(2,1)S(1)}, bf16[64,1024]{1,0:T(8,128)(2,1)S(1)}, u32[]{:S(2)}, u32[]{:S(2)}) collective-permute-start(bf16[64,1024]{1,0:T(8,128)(2,1)S(1)} %collective-permute-done.3), channel_id=1, source_target_pairs={{0,1},{1,2},{2,3},{3,4},{4,5},{5,6},{6,7},{7,8},{8,9},{9,10},{10,1... | collective-permute-start | bytes 393224 | tf_op jit(solution)/shard_map/ppermute | solution.py:42
  111.8 9.5 %collective-permute-start.5 = (bf16[64,1024]{1,0:T(8,128)(2,1)S(1)}, bf16[64,1024]{1,0:T(8,128)(2,1)S(1)}, u32[]{:S(2)}, u32[]{:S(2)}) collective-permute-start(bf16[64,1024]{1,0:T(8,128)(2,1)S(1)} %collective-permute-done.4), channel_id=1, source_target_pairs={{0,1},{1,2},{2,3},{3,4},{4,5},{5,6},{6,7},{7,8},{8,9},{9,10},{10,1... | collective-permute-start | bytes 393224 | tf_op jit(solution)/shard_map/ppermute | solution.py:42
  121.4 8.5 %collective-permute-start.6 = (bf16[64,1024]{1,0:T(8,128)(2,1)S(1)}, bf16[64,1024]{1,0:T(8,128)(2,1)S(1)}, u32[]{:S(2)}, u32[]{:S(2)}) collective-permute-start(bf16[64,1024]{1,0:T(8,128)(2,1)S(1)} %collective-permute-done.5), channel_id=1, source_target_pairs={{0,1},{1,2},{2,3},{3,4},{4,5},{5,6},{6,7},{7,8},{8,9},{9,10},{10,1... | collective-permute-start | bytes 393224 | tf_op jit(solution)/shard_map/ppermute | solution.py:42
  129.9 8.1 %collective-permute-start.7 = (bf16[64,1024]{1,0:T(8,128)(2,1)S(1)}, bf16[64,1024]{1,0:T(8,128)(2,1)S(1)}, u32[]{:S(2)}, u32[]{:S(2)}) collective-permute-start(bf16[64,1024]{1,0:T(8,128)(2,1)S(1)} %collective-permute-done.6), channel_id=1, source_target_pairs={{0,1},{1,2},{2,3},{3,4},{4,5},{5,6},{6,7},{7,8},{8,9},{9,10},{10,1... | collective-permute-start | bytes 393224 | tf_op jit(solution)/shard_map/ppermute | solution.py:42
  137.9 8.1 %collective-permute-start.8 = (bf16[64,1024]{1,0:T(8,128)(2,1)S(1)}, bf16[64,1024]{1,0:T(8,128)(2,1)S(1)}, u32[]{:S(2)}, u32[]{:S(2)}) collective-permute-start(bf16[64,1024]{1,0:T(8,128)(2,1)S(1)} %collective-permute-done.7), channel_id=1, source_target_pairs={{0,1},{1,2},{2,3},{3,4},{4,5},{5,6},{6,7},{7,8},{8,9},{9,10},{10,1... | collective-permute-start | bytes 393224 | tf_op jit(solution)/shard_map/ppermute | solution.py:42
  146.0 8.1 %collective-permute-start.9 = (bf16[64,1024]{1,0:T(8,128)(2,1)S(1)}, bf16[64,1024]{1,0:T(8,128)(2,1)S(1)}, u32[]{:S(2)}, u32[]{:S(2)}) collective-permute-start(bf16[64,1024]{1,0:T(8,128)(2,1)S(1)} %collective-permute-done.8), channel_id=1, source_target_pairs={{0,1},{1,2},{2,3},{3,4},{4,5},{5,6},{6,7},{7,8},{8,9},{9,10},{10,1... | collective-permute-start | bytes 393224 | tf_op jit(solution)/shard_map/ppermute | solution.py:42
  154.1 9.0 %collective-permute-start.10 = (bf16[64,1024]{1,0:T(8,128)(2,1)S(1)}, bf16[64,1024]{1,0:T(8,128)(2,1)S(1)}, u32[]{:S(2)}, u32[]{:S(2)}) collective-permute-start(bf16[64,1024]{1,0:T(8,128)(2,1)S(1)} %collective-permute-done.9), channel_id=1, source_target_pairs={{0,1},{1,2},{2,3},{3,4},{4,5},{5,6},{6,7},{7,8},{8,9},{9,10},{10,1... | collective-permute-start | bytes 393224 | tf_op jit(solution)/shard_map/ppermute | solution.py:42
  160.4 201.3 %all-gather.5.cloned.1.call-start = ((), (), s32[]{:S(2)}) async-start(), calls=%async_computation.6 | async-start | bytes 2228224 | tf_op jit(solution)/shard_map/all_gather | solution.py:81
  163.1 10.3 %collective-permute-start.11 = (bf16[64,1024]{1,0:T(8,128)(2,1)S(1)}, bf16[64,1024]{1,0:T(8,128)(2,1)S(1)}, u32[]{:S(2)}, u32[]{:S(2)}) collective-permute-start(bf16[64,1024]{1,0:T(8,128)(2,1)S(1)} %collective-permute-done.10), channel_id=1, source_target_pairs={{0,1},{1,2},{2,3},{3,4},{4,5},{5,6},{6,7},{7,8},{8,9},{9,10},{10,1... | collective-permute-start | bytes 393224 | tf_op jit(solution)/shard_map/ppermute | solution.py:42
  173.4 11.1 %collective-permute-start.12 = (bf16[64,1024]{1,0:T(8,128)(2,1)S(1)}, bf16[64,1024]{1,0:T(8,128)(2,1)S(1)}, u32[]{:S(2)}, u32[]{:S(2)}) collective-permute-start(bf16[64,1024]{1,0:T(8,128)(2,1)S(1)} %collective-permute-done.11), channel_id=1, source_target_pairs={{0,1},{1,2},{2,3},{3,4},{4,5},{5,6},{6,7},{7,8},{8,9},{9,10},{10,1... | collective-permute-start | bytes 393224 | tf_op jit(solution)/shard_map/ppermute | solution.py:42
  184.5 9.7 %collective-permute-start.13 = (bf16[64,1024]{1,0:T(8,128)(2,1)S(1)}, bf16[64,1024]{1,0:T(8,128)(2,1)S(1)}, u32[]{:S(2)}, u32[]{:S(2)}) collective-permute-start(bf16[64,1024]{1,0:T(8,128)(2,1)S(1)} %collective-permute-done.12), channel_id=1, source_target_pairs={{0,1},{1,2},{2,3},{3,4},{4,5},{5,6},{6,7},{7,8},{8,9},{9,10},{10,1... | collective-permute-start | bytes 393224 | tf_op jit(solution)/shard_map/ppermute | solution.py:42
  194.2 8.8 %collective-permute-start.14 = (bf16[64,1024]{1,0:T(8,128)(2,1)S(1)}, bf16[64,1024]{1,0:T(8,128)(2,1)S(1)}, u32[]{:S(2)}, u32[]{:S(2)}) collective-permute-start(bf16[64,1024]{1,0:T(8,128)(2,1)S(1)} %collective-permute-done.13), channel_id=1, source_target_pairs={{0,1},{1,2},{2,3},{3,4},{4,5},{5,6},{6,7},{7,8},{8,9},{9,10},{10,1... | collective-permute-start | bytes 393224 | tf_op jit(solution)/shard_map/ppermute | solution.py:42
  282.8 3.6 slice-start
  (1 other events, 0.9 us)
Sparse Core Ops, SparseCore 0:
  65.3 68.5 reduce-scatter.6
  136.8 71.8 all-gather.2
  211.8 76.4 reduce-scatter.4
  290.4 71.2 all-gather.4
